TPU v7x, 32 devices: a whole 2x2x4 slice. The times are simulated.
32 devices in a mesh: row: 16 (over z, y, core), col: 2 (over x).
Axes of the slice: x: 2, y: 2, z: 4, core: 2. Of those that a mesh axis runs over, the one named last changes fastest.
Arguments:
- jacobian: bfloat16 [512, 256, 128], P(('col', 'row')), may hold values from -1.5 to 1.5
- weights: bfloat16 [32, 512, 256], P('row', 'col'), may hold values from 0.25 to 4
- panel_weights: bfloat16 [512, 256], P(('col', 'row')), may hold values from 0.25 to 4
- damping: float32 [32, 128], P('row'), may hold values from 0.01 to 1
- panel_inverse: float32 [128, 128], replicated, may hold values from -0.12 to 0.12
Outputs:
- schur: float32 [4096, 65536], P('row', 'col')
All inputs are finite; a program needn't handle non-finite values.
Results may differ from a plain program's by a relative error of at most 0.0022.
Values may be sent and summed in bfloat16 or wider, within the bound.
No kernel may reach another device: no remote copies, remote signals or barrier semaphores. Data moves between devices by JAX's collectives and lax.ppermute only.
A program may use at most 128 MiB of HBM per device.

v0:
```python
import jax
import jax.numpy as jnp
from jax import lax
from jax.sharding import PartitionSpec as P

HIGHEST = lax.Precision.HIGHEST


def broadcast(value, axis, root):
    mine = lax.axis_index(axis) == root
    return lax.psum(jnp.where(mine, value, jnp.zeros_like(value)), axis)


def shards(jacobian, weights, panel_weights, damping, panel_inverse):
    per_dev, sample_rows, param_width = jacobian.shape
    slab_rows, col_block, _ = weights.shape
    row_count = lax.axis_size("row")
    col_count = lax.axis_size("col")
    row_index = lax.axis_index("row")
    col_index = lax.axis_index("col")
    station_total = col_block * col_count
    panel_id = station_total - 1
    slab_ids = row_index * slab_rows + jnp.arange(slab_rows, dtype=jnp.int32)
    col_base = col_index * col_block
    col_ids = col_base + jnp.arange(col_block, dtype=jnp.int32)
    station_piece = lax.all_gather(jacobian, "row", axis=0, tiled=True)
    how_many = station_piece.shape[0]
    piece_ids = col_base + jnp.arange(how_many, dtype=jnp.int32)
    self_pair = slab_ids[:, None] == piece_ids[None, :]
    scaled = weights.astype(jnp.float32)[..., None] * station_piece.astype(jnp.float32)[None]
    scaled = jnp.where(self_pair[:, :, None, None], 0.0, scaled).astype(jnp.bfloat16)
    gram_part = jnp.einsum(
        "ijra,jrb->iab", scaled, station_piece, preferred_element_type=jnp.float32
    )
    gathered = station_piece
    scaled_all = scaled
    gram_part, gathered, scaled_all = (gram_part, gathered, scaled_all)
    home_col = row_index * slab_rows // col_block
    offset = row_index * slab_rows % col_block
    my_slab = lax.dynamic_slice_in_dim(gathered, offset, slab_rows, 0)
    slab_jac = broadcast(my_slab, "col", home_col)
    coupling = jnp.einsum(
        "ijra,irb->iajb", scaled_all, slab_jac, preferred_element_type=jnp.float32
    )
    gram_sum = lax.psum(gram_part, "col")
    identity = jnp.eye(param_width, dtype=jnp.float32)
    diag_block = (
        gram_sum + identity[None] * (jnp.diagonal(gram_sum, axis1=1, axis2=2) * damping)[:, None, :]
    )
    on_self = slab_ids[:, None] == col_ids[None, :]
    hessian = jnp.where(on_self[:, None, :, None], diag_block[:, :, None, :], coupling)
    local_factor = jnp.einsum(
        "iac,cb->iab",
        hessian[:, :, col_block - 1, :],
        panel_inverse,
        precision=HIGHEST,
        preferred_element_type=jnp.float32,
    )
    panel_factor, panel_jac = (
        broadcast(local_factor.astype(jnp.bfloat16), "col", col_count - 1).astype(
            local_factor.dtype
        ),
        broadcast(gathered[col_block - 1], "col", col_count - 1),
    )
    own_ids = (col_index * row_count + row_index) * per_dev + jnp.arange(per_dev, dtype=jnp.int32)
    scaled_rows = panel_weights.astype(jnp.float32)[..., None] * jacobian.astype(jnp.float32)
    scaled_rows = jnp.where((own_ids == panel_id)[:, None, None], 0.0, scaled_rows).astype(
        jnp.bfloat16
    )
    row_part = jnp.einsum("jra,rb->jab", scaled_rows, panel_jac, preferred_element_type=jnp.float32)
    station_piece = lax.all_gather(row_part.astype(jnp.bfloat16), "row", axis=0, tiled=True).astype(
        jnp.float32
    )
    how_many = station_piece.shape[0]
    current = lax.slice_in_dim(hessian, 0, how_many, axis=2)
    correction = jnp.einsum(
        "iac,jcb->iajb",
        panel_factor,
        station_piece,
        precision=HIGHEST,
        preferred_element_type=jnp.float32,
    )
    piece_ids = col_base + jnp.arange(how_many, dtype=jnp.int32)
    result = jnp.where(
        (piece_ids == panel_id)[None, None, :, None],
        panel_factor[:, :, None, :],
        current - correction,
    )
    return result.reshape(slab_rows * param_width, how_many * param_width)


def solution(mesh):
    return jax.shard_map(
        shards,
        mesh=mesh,
        in_specs=(
            P(("col", "row"), None, None),
            P("row", "col", None),
            P(("col", "row"), None),
            P("row", None),
            P(),
        ),
        out_specs=P("row", "col"),
        check_vma=False,
    )
```

profile of v0, /device:TPU:0, one launch (start us, length us, event | category | flops | bytes accessed | tf_op | source)
XLA Modules:
  0.0 486.4 jit_solution(10741653485367392175)
XLA Ops:
  6.5 0.0 copy-start
  6.5 0.0 all-gather.3.cloned.1.call-start
  6.5 0.7 all-gather.3.cloned.1.call-update
  7.3 0.0 all-reduce.5.cloned.1.call-start
  7.3 1.0 convert_element_type.35
  8.4 0.1 broadcast_compare_fusion
  8.5 130.7 %all-gather.3.cloned.1.call-done = bf16[256,256,128]{2,1,0:T(8,128)(2,1)} async-done(((bf16[16,256,128]{2,1,0:T(8,128)(2,1)}), bf16[256,256,128]{2,1,0:T(8,128)(2,1)}) %all-gather.3.cloned.1.call-update) | async-done | bytes 16777232 | tf_op jit(solution)/shard_map/all_gather | solution.py:26
  139.1 0.9 constant_dynamic-slice_fusion
  140.1 0.1 copy.53
  140.2 9.4 %convert_element_type.36 = f32[256,256,128]{2,1,0:T(8,128)S(1)} convert(bf16[256,256,128]{2,1,0:T(8,128)(2,1)} %all-gather.3.cloned.1.call-done) | non-fusion elementwise | flops 8388608 | bytes 50331648 | tf_op jit(solution)/shard_map/convert_element_type | solution.py:30
  149.6 0.0 copy-start.1
  149.6 11.7 %copy-done.1 = f32[256,256,128]{2,1,0:T(8,128)} copy-done((f32[256,256,128]{2,1,0:T(8,128)}, f32[256,256,128]{2,1,0:T(8,128)S(1)}, u32[]{:S(2)}) %copy-start.1) | copy-done | bytes 33554456
  161.3 0.0 copy-start.5
  161.3 47.9 %fusion.12 = f32[2,128,128]{2,1,0:T(8,128)} fusion(bf16[256,256,128]{2,1,0:T(8,128)(2,1)} %all-gather.3.cloned.1.call-done, f32[256,256,128]{2,1,0:T(8,128)S(1)} %convert_element_type.36, f32[2,256,256]{2,1,0:T(8,128)S(1)} %convert_element_type.35, pred[2,256]{1,0:T(4,128)(4,1)S(1)} %broadcast_compare_fusion), kind=kOutput, calls=%fused_computation.19 | convolution fusion | flops 4345298944 | bytes 50987520 | tf_op jit(solution)/shard_map/ijra,jrb->iab/dot_general | solution.py:32
  209.2 0.0 all-reduce.5.cloned.1.call-update
  209.2 0.0 all-reduce.7.cloned.1.call-start
  209.2 0.7 broadcast_select_fusion
  209.9 0.0 all-reduce.7.cloned.1.call-update
  209.9 0.0 all-reduce.9.cloned.1.call-start
  210.0 1.5 fusion.20
  211.5 17.5 %all-reduce.5.cloned.1.call-done = f32[2,128,128]{2,1,0:T(8,128)} async-done(((f32[2,128,128]{2,1,0:T(8,128)}), f32[2,128,128]{2,1,0:T(8,128)}) %all-reduce.5.cloned.1.call-update) | async-done | bytes 131088 | tf_op jit(solution)/shard_map/psum | solution.py:45
  228.9 5.5 %copy.37 = f32[2,128,128]{0,2,1:T(8,128)} copy(f32[2,128,128]{2,1,0:T(8,128)} %all-reduce.5.cloned.1.call-done) | data formatting | bytes 262144 | tf_op jit(solution)/shard_map/psum | solution.py:45
  234.4 1.8 gather_fusion
  236.2 0.1 copy.38
  236.3 0.0 copy-done.5
  236.3 0.9 multiply_add_fusion
  237.2 0.1 copy.39
  237.3 0.0 copy-start.4
  237.3 0.0 copy-start.3
  237.4 15.3 %all-reduce.7.cloned.1.call-done = bf16[2,256,128]{1,2,0:T(8,128)(2,1)} async-done(((bf16[2,256,128]{1,2,0:T(8,128)(2,1)}), bf16[2,256,128]{1,2,0:T(8,128)(2,1)}) %all-reduce.7.cloned.1.call-update) | async-done | bytes 131088 | tf_op jit(solution)/shard_map/psum | solution.py:11
  252.7 23.6 %bitcast_select_fusion = f32[2,128,256,128]{1,3,2,0:T(8,128)S(1)} fusion(f32[2,128,128]{1,2,0:T(8,128)S(1)} %copy.39, pred[2,256]{1,0:T(4,128)(4,1)S(1)} %broadcast_compare_fusion, f32[256,256,128]{2,1,0:T(8,128)} %copy-done.1, f32[2,256,256]{2,1,0:T(8,128)S(1)} %convert_element_type.35, bf16[2,256,128]{1,2,0:T(8,128)(2,1)} %all-reduce.7.cloned.1.call-done), kind=kOutput, calls=%fused_computation.5 | convolution fusion | flops 4353687552 | bytes 67895808 | tf_op jit(solution)/shard_map/ijra,irb->iajb/dot_general | solution.py:42
  276.3 0.0 copy-start.2
  276.3 11.7 %copy-done.2 = f32[2,128,256,128]{1,3,2,0:T(8,128)} copy-done((f32[2,128,256,128]{1,3,2,0:T(8,128)}, f32[2,128,256,128]{1,3,2,0:T(8,128)S(1)}, u32[]{:S(2)}) %copy-start.2) | copy-done | bytes 33554456
  288.0 0.0 copy-done
  288.0 1.0 fusion.15
  289.0 0.0 all-reduce.9.cloned.1.call-update
  289.1 0.2 all-gather.5.cloned.1.call-start
  289.3 0.0 copy-done.4
  289.3 21.5 %all-reduce.9.cloned.1.call-done = (bf16[2,128,128]{2,1,0:T(8,128)(2,1)}, bf16[256,128]{1,0:T(8,128)(2,1)}) async-done(((bf16[2,128,128]{2,1,0:T(8,128)(2,1)}, bf16[256,128]{1,0:T(8,128)(2,1)}), (bf16[2,128,128]{2,1,0:T(8,128)(2,1)}, bf16[256,128]{1,0:T(8,128)(2,1)})) %all-reduce.9.cloned.1.call-update) | async-done | bytes 131088 | tf_op jit(solution)/shard_map/psum | solution.py:11
  310.8 0.0 copy-done.3
  310.8 2.9 convolution_convert_fusion
  313.7 0.0 all-gather.5.cloned.1.call-update
  313.7 0.9 copy.42
  314.7 74.1 %all-gather.5.cloned.1.call-done = bf16[256,128,128]{2,1,0:T(8,128)(2,1)} async-done(((bf16[16,128,128]{2,1,0:T(8,128)(2,1)}), bf16[256,128,128]{2,1,0:T(8,128)(2,1)}) %all-gather.5.cloned.1.call-update) | async-done | bytes 8388624 | tf_op jit(solution)/shard_map/all_gather | solution.py:71
  388.8 28.2 %subtract_select_fusion = f32[2,128,256,128]{1,3,2,0:T(8,128)} fusion(f32[2,128,256,128]{1,3,2,0:T(8,128)} %copy-done.2, f32[2,128,128]{1,2,0:T(8,128)S(1)} %copy.42, pred[256]{0:T(512)(128)(4,1)S(1)} %broadcast_compare_fusion.1, bf16[256,128,128]{2,1,0:T(8,128)(2,1)} %all-gather.5.cloned.1.call-done, bf16[2,128,128]{2,1,0:T(8,128)(2,1)} %get-tuple-element.5), kind=kOutput, calls=%fused_computation.6 | convolution fusion | flops 2164260864 | bytes 75694336 | tf_op jit(solution)/shard_map/iac,jcb->iajb/dot_general | solution.py:76
  417.0 31.1 %copy.45 = f32[2,128,256,128]{3,2,1,0:T(8,128)} copy(f32[2,128,256,128]{1,3,2,0:T(8,128)} %subtract_select_fusion) | data formatting | bytes 67108864 | tf_op jit(solution)/shard_map/jit(_where)/select_n | solution.py:84
  448.1 31.8 %copy.56 = f32[32,8,256,128]{3,1,2,0:T(8,128)} copy(f32[32,8,256,128]{3,2,1,0:T(8,128)} %bitcast.47) | data formatting | bytes 67108864
  (8 shorter events, 0.1 us)
Async XLA Ops:
  6.5 281.5 %copy-start = (f32[128,128]{1,0:T(8,128)S(1)}, f32[128,128]{1,0:T(8,128)}, u32[]{:S(2)}) copy-start(f32[128,128]{1,0:T(8,128)} %param.9) | copy-start | bytes 196612
  6.5 132.6 %all-gather.3.cloned.1.call-start = ((), (), s32[]{:S(2)}) async-start(), calls=%async_computation | async-start | bytes 17825792 | tf_op jit(solution)/shard_map/all_gather | solution.py:26
  7.3 221.7 %all-reduce.5.cloned.1.call-start = ((), (), s32[]{:S(2)}) async-start(), calls=%async_computation.1 | async-start | bytes 262144 | tf_op jit(solution)/shard_map/psum | solution.py:45
  149.6 11.7 %copy-start.1 = (f32[256,256,128]{2,1,0:T(8,128)}, f32[256,256,128]{2,1,0:T(8,128)S(1)}, u32[]{:S(2)}) copy-start(f32[256,256,128]{2,1,0:T(8,128)S(1)} %convert_element_type.36) | copy-start | bytes 100663296
  161.3 75.0 %copy-start.5 = (f32[2,128]{1,0:T(2,128)S(1)}, f32[2,128]{1,0:T(2,128)}, u32[]{:S(2)}) copy-start(f32[2,128]{1,0:T(2,128)} %param.8) | copy-start | bytes 3076
  209.2 43.5 %all-reduce.7.cloned.1.call-start = ((), (), s32[]{:S(2)}) async-start(), calls=%async_computation.2 | async-start | bytes 262144 | tf_op jit(solution)/shard_map/psum | solution.py:11
  209.9 100.9 %all-reduce.9.cloned.1.call-start = ((), (), s32[]{:S(2)}) async-start(), calls=%async_computation.4 | async-start | bytes 262144 | tf_op jit(solution)/shard_map/psum | solution.py:11
  237.3 52.0 %copy-start.4 = (bf16[16,256]{1,0:T(8,128)(2,1)S(1)}, bf16[16,256]{1,0:T(8,128)(2,1)}, u32[]{:S(2)}) copy-start(bf16[16,256]{1,0:T(8,128)(2,1)} %param.7) | copy-start | bytes 24580
  237.3 73.5 %copy-start.3 = (bf16[16,256,128]{2,1,0:T(8,128)(2,1)S(1)}, bf16[16,256,128]{2,1,0:T(8,128)(2,1)}, u32[]{:S(2)}) copy-start(bf16[16,256,128]{2,1,0:T(8,128)(2,1)} %param.5) | copy-start | bytes 3145732
  276.3 11.7 %copy-start.2 = (f32[2,128,256,128]{1,3,2,0:T(8,128)}, f32[2,128,256,128]{1,3,2,0:T(8,128)S(1)}, u32[]{:S(2)}) copy-start(f32[2,128,256,128]{1,3,2,0:T(8,128)S(1)} %bitcast_select_fusion) | copy-start | bytes 100663296
  289.1 99.7 %all-gather.5.cloned.1.call-start = ((), (), s32[]{:S(2)}) async-start(), calls=%async_computation.3 | async-start | bytes 8912896 | tf_op jit(solution)/shard_map/all_gather | solution.py:71
Sparse Core Ops, SparseCore 0:
  9.5 129.5 all-gather.2
  209.3 19.5 all-reduce.4
  231.2 21.4 all-reduce.6
  289.2 21.5 all-reduce.8
  313.8 74.8 all-gather.4
where the time goes:
time: 488 us; the launch traced here: 486 us
  waiting for transfers between devices  260 us (53%)
  matrix products  104 us (21%)
  local copies, waits for them, and re-layouts  95.7 us (20%)
  other arithmetic  13.6 us (3%)
  between operations  13.3 us (3%)
    all_gather x1, waiting for transfers between devices, shards(): station_piece = lax.all_gather(jacobian, 'row', axis=0, tiled=True)  131 us
    all_gather x1, waiting for transfers between devices, shards(): lax.all_gather(row_part.astype(jnp.bfloat16), 'row', axis=0, tiled=True)  74.1 us
    unnamed x14, local copies, waits for them, and re-layouts  55.3 us
    dot_general x1, matrix products, shards(): jnp.einsum('ijra,jrb->iab', scaled, station_piece, preferred_element_type...  47.9 us
    psum x2, waiting for transfers between devices, broadcast(): return lax.psum(jnp.where(mine, value, jnp.zeros_like(value)), axis)  36.8 us
    select_n x1, local copies, waits for them, and re-layouts, shards(): jnp.where((piece_ids == panel_id)[None, None, :, None], panel_factor[:, :...  31.1 us
    dot_general x1, matrix products, shards(): jnp.einsum('iac,jcb->iajb', panel_factor, station_piece, precision=HIGHES...  28.2 us
    dot_general x1, matrix products, shards(): jnp.einsum('ijra,irb->iajb', scaled_all, slab_jac, preferred_element_type...  23.6 us
  transfers between devices with their start and end apart: 5, of which 5 were waited for; matrix products, arithmetic and copies ran while one was open for 3% of the time, Pallas kernels for 0%

commit v1 on v0

--- a/solution.py
+++ b/solution.py
@@ -4,6 +4,28 @@
 from jax.sharding import PartitionSpec as P
 
 HIGHEST = lax.Precision.HIGHEST
+
+
+def joined_along(tiles, dim):
+    shape = list(tiles.shape[1:])
+    shape[dim] *= tiles.shape[0]
+    return jnp.moveaxis(tiles, 0, dim).reshape(shape)
+
+
+def grow_blocks(x, axis):
+    size = lax.axis_size(axis)
+    blocks = x[None]
+    for level in range(size.bit_length() - 1):
+        bit = 1 << level
+        received = lax.ppermute(blocks, axis, [(i, i ^ bit) for i in range(size)])
+        both = jnp.stack([blocks, received])
+        upper = lax.axis_index(axis) >> level & 1
+        blocks = jnp.where(upper == 0, both, both[::-1]).reshape(-1, *x.shape)
+    return blocks
+
+
+def doubled_up(value, axis, dim):
+    return joined_along(grow_blocks(value, axis), dim)
 
 
 def broadcast(value, axis, root):
@@ -68,9 +90,7 @@
         jnp.bfloat16
     )
     row_part = jnp.einsum("jra,rb->jab", scaled_rows, panel_jac, preferred_element_type=jnp.float32)
-    station_piece = lax.all_gather(row_part.astype(jnp.bfloat16), "row", axis=0, tiled=True).astype(
-        jnp.float32
-    )
+    station_piece = doubled_up(row_part.astype(jnp.bfloat16), "row", 0).astype(jnp.float32)
     how_many = station_piece.shape[0]
     current = lax.slice_in_dim(hessian, 0, how_many, axis=2)
     correction = jnp.einsum(

time: 488 us -> 697 us (1.43)
  waiting for transfers between devices: 260 us -> 437 us
  other arithmetic: 13.6 us -> 41.6 us
    ppermute x0 -> x4, waiting for transfers between devices: none -> 251 us  [grow_blocks(): received = lax.ppermute(blocks, axis, [(i, i ^ bit) for i in range(size)])]
    all_gather x1 -> x0, waiting for transfers between devices: 74.1 us -> none  [shards(): lax.all_gather(row_part.astype(jnp.bfloat16), 'row', axis=0, tiled=True)]
    select_n x0 -> x3, other arithmetic: none -> 18.6 us  [grow_blocks(): blocks = jnp.where(upper == 0, both, both[::-1]).reshape(-1, *x.shape)]
    another operation x0 -> x5, other arithmetic: none -> 10.4 us  [grow_blocks(): both = jnp.stack([blocks, received])]
    unnamed x14 -> x20, local copies, waits for them, and re-layouts: 55.3 us -> 55.4 us
  transfers between devices with their start and end apart: 5 -> 8, of which waited for: 5 -> 8; matrix products, arithmetic and copies ran while one was open for 3% -> 2% of each run, Pallas kernels for 0% -> 0%
where the time goes in v1:
time: 697 us; the launch traced here: 696 us
  waiting for transfers between devices  437 us (63%)
  matrix products  103 us (15%)
  local copies, waits for them, and re-layouts  95.1 us (14%)
  other arithmetic  41.6 us (6%)
  between operations  13.4 us (2%)
    ppermute x4, waiting for transfers between devices, grow_blocks(): received = lax.ppermute(blocks, axis, [(i, i ^ bit) for i in range(size)])  251 us
    all_gather x1, waiting for transfers between devices, shards(): station_piece = lax.all_gather(jacobian, 'row', axis=0, tiled=True)  131 us
    unnamed x20, local copies, waits for them, and re-layouts  55.4 us
    dot_general x1, matrix products, shards(): jnp.einsum('ijra,jrb->iab', scaled, station_piece, preferred_element_type...  47.9 us
    psum x2, waiting for transfers between devices, broadcast(): return lax.psum(jnp.where(mine, value, jnp.zeros_like(value)), axis)  37.8 us
    select_n x1, local copies, waits for them, and re-layouts, shards(): jnp.where((piece_ids == panel_id)[None, None, :, None], panel_factor[:, :...  31.2 us
    dot_general x1, matrix products, shards(): jnp.einsum('iac,jcb->iajb', panel_factor, station_piece, precision=HIGHES...  28.2 us
    dot_general x1, matrix products, shards(): jnp.einsum('ijra,irb->iajb', scaled_all, slab_jac, preferred_element_type...  23.6 us
  transfers between devices with their start and end apart: 8, of which 8 were waited for; matrix products, arithmetic and copies ran while one was open for 2% of the time, Pallas kernels for 0%

profile of v1, /device:TPU:0, one launch (start us, length us, event | category | flops | bytes accessed | tf_op | source)
XLA Modules:
  0.0 695.9 jit_solution(18171121005672023169)
XLA Ops:
  6.5 0.7 all-gather.2.cloned.1.call-update
  7.3 0.0 all-reduce.5.cloned.1.call-start
  7.3 1.0 convert_element_type.35
  8.4 0.1 broadcast_compare_fusion
  8.5 130.7 %all-gather.2.cloned.1.call-done = bf16[256,256,128]{2,1,0:T(8,128)(2,1)} async-done(((bf16[16,256,128]{2,1,0:T(8,128)(2,1)}), bf16[256,256,128]{2,1,0:T(8,128)(2,1)}) %all-gather.2.cloned.1.call-update) | async-done | bytes 16777232 | tf_op jit(solution)/shard_map/all_gather | solution.py:48
  139.1 0.9 constant_dynamic-slice_fusion
  140.1 0.1 copy.55
  140.2 9.4 %convert_element_type.36 = f32[256,256,128]{2,1,0:T(8,128)S(1)} convert(bf16[256,256,128]{2,1,0:T(8,128)(2,1)} %all-gather.2.cloned.1.call-done) | non-fusion elementwise | flops 8388608 | bytes 50331648 | tf_op jit(solution)/shard_map/convert_element_type | solution.py:52
  149.6 11.7 %copy-done.2 = f32[256,256,128]{2,1,0:T(8,128)} copy-done((f32[256,256,128]{2,1,0:T(8,128)}, f32[256,256,128]{2,1,0:T(8,128)S(1)}, u32[]{:S(2)}) %copy-start.2) | copy-done | bytes 33554456
  161.3 47.9 %fusion.11 = f32[2,128,128]{2,1,0:T(8,128)} fusion(bf16[256,256,128]{2,1,0:T(8,128)(2,1)} %all-gather.2.cloned.1.call-done, f32[256,256,128]{2,1,0:T(8,128)S(1)} %convert_element_type.36, f32[2,256,256]{2,1,0:T(8,128)S(1)} %convert_element_type.35, pred[2,256]{1,0:T(4,128)(4,1)S(1)} %broadcast_compare_fusion), kind=kOutput, calls=%fused_computation.25 | convolution fusion | flops 4345298944 | bytes 50987520 | tf_op jit(solution)/shard_map/ijra,jrb->iab/dot_general | solution.py:54
  209.2 0.0 all-reduce.5.cloned.1.call-update
  209.2 0.0 all-reduce.7.cloned.1.call-start
  209.2 0.7 broadcast_select_fusion
  209.9 0.0 all-reduce.7.cloned.1.call-update
  209.9 0.0 all-reduce.9.cloned.1.call-start
  210.0 1.5 fusion.21
  211.4 17.5 %all-reduce.5.cloned.1.call-done = f32[2,128,128]{2,1,0:T(8,128)} async-done(((f32[2,128,128]{2,1,0:T(8,128)}), f32[2,128,128]{2,1,0:T(8,128)}) %all-reduce.5.cloned.1.call-update) | async-done | bytes 131088 | tf_op jit(solution)/shard_map/psum | solution.py:67
  228.9 5.6 copy.39
  234.5 1.8 gather_fusion
  236.3 0.1 copy.40
  236.4 0.1 copy.41
  236.5 16.1 %all-reduce.7.cloned.1.call-done = bf16[2,256,128]{1,2,0:T(8,128)(2,1)} async-done(((bf16[2,256,128]{1,2,0:T(8,128)(2,1)}), bf16[2,256,128]{1,2,0:T(8,128)(2,1)}) %all-reduce.7.cloned.1.call-update) | async-done | bytes 131088 | tf_op jit(solution)/shard_map/psum | solution.py:33
  252.7 23.6 %bitcast_select_fusion = f32[2,128,256,128]{1,3,2,0:T(8,128)S(1)} fusion(f32[2,128,128]{1,2,0:T(8,128)S(1)} %copy.41, pred[2,256]{1,0:T(4,128)(4,1)S(1)} %broadcast_compare_fusion, f32[256,256,128]{2,1,0:T(8,128)} %copy-done.2, f32[2,256,256]{2,1,0:T(8,128)S(1)} %convert_element_type.35, bf16[2,256,128]{1,2,0:T(8,128)(2,1)} %all-reduce.7.cloned.1.call-done), kind=kOutput, calls=%fused_computation.5 | convolution fusion | flops 4353687552 | bytes 67895808 | tf_op jit(solution)/shard_map/ijra,irb->iajb/dot_general | solution.py:64
  276.3 11.7 %copy-done.3 = f32[2,128,256,128]{1,3,2,0:T(8,128)} copy-done((f32[2,128,256,128]{1,3,2,0:T(8,128)}, f32[2,128,256,128]{1,3,2,0:T(8,128)S(1)}, u32[]{:S(2)}) %copy-start.3) | copy-done | bytes 33554456
  288.0 1.0 fusion.14
  289.0 0.0 all-reduce.9.cloned.1.call-update
  289.1 21.7 %all-reduce.9.cloned.1.call-done = (bf16[2,128,128]{2,1,0:T(8,128)(2,1)}, bf16[256,128]{1,0:T(8,128)(2,1)}) async-done(((bf16[2,128,128]{2,1,0:T(8,128)(2,1)}, bf16[256,128]{1,0:T(8,128)(2,1)}), (bf16[2,128,128]{2,1,0:T(8,128)(2,1)}, bf16[256,128]{1,0:T(8,128)(2,1)})) %all-reduce.9.cloned.1.call-update) | async-done | bytes 131088 | tf_op jit(solution)/shard_map/psum | solution.py:33
  310.8 2.2 convolution_convert_fusion
  312.9 0.1 collective-permute-start
  313.0 1.9 collective-permute-done
  314.9 0.1 pad_maximum_fusion.3
  315.0 0.6 fusion.19
  315.6 1.5 collective-permute-start.1
  317.2 23.7 %collective-permute-done.1 = bf16[2,16,128,128]{3,2,1,0:T(8,128)(2,1)S(1)} collective-permute-done((bf16[2,16,128,128]{3,2,1,0:T(8,128)(2,1)S(1)}, bf16[2,16,128,128]{3,2,1,0:T(8,128)(2,1)S(1)}, u32[]{:S(2)}, u32[]{:S(2)}) %collective-permute-start.1) | collective-permute-done | bytes 1048608 | tf_op jit(solution)/shard_map/ppermute | solution.py:20
  340.9 0.2 pad_maximum_fusion.2
  341.1 0.6 reverse_select_fusion.2
  341.7 1.5 collective-permute-start.2
  343.2 45.5 %collective-permute-done.2 = bf16[4,16,128,128]{3,2,1,0:T(8,128)(2,1)} collective-permute-done((bf16[4,16,128,128]{3,2,1,0:T(8,128)(2,1)S(1)}, bf16[4,16,128,128]{3,2,1,0:T(8,128)(2,1)}, u32[]{:S(2)}, u32[]{:S(2)}) %collective-permute-start.2) | collective-permute-done | bytes 2097184 | tf_op jit(solution)/shard_map/ppermute | solution.py:20
  388.7 2.0 pad_maximum_fusion.1
  390.7 3.1 reverse_select_fusion.1
  393.8 2.4 collective-permute-start.3
  396.2 0.1 copy.44
  396.3 179.4 %collective-permute-done.3 = bf16[8,16,128,128]{3,2,1,0:T(8,128)(2,1)} collective-permute-done((bf16[8,16,128,128]{3,2,1,0:T(8,128)(2,1)}, bf16[8,16,128,128]{3,2,1,0:T(8,128)(2,1)}, u32[]{:S(2)}, u32[]{:S(2)}) %collective-permute-start.3) | collective-permute-done | bytes 4194336 | tf_op jit(solution)/shard_map/ppermute | solution.py:20
  575.8 7.5 %pad_maximum_fusion = bf16[2,8,16,128,128]{4,3,2,1,0:T(8,128)(2,1)} fusion(bf16[1,8,16,128,128]{4,3,2,1,0:T(8,128)(2,1)} %bitcast.25, bf16[1,8,16,128,128]{4,3,2,1,0:T(8,128)(2,1)} %bitcast.23), kind=kLoop, calls=%fused_computation.17 | loop fusion | flops 4194304 | bytes 16777216 | tf_op jit(solution)/shard_map/stack | solution.py:21
  583.2 14.9 %reverse_select_fusion = bf16[2,8,16,128,128]{4,3,2,1,0:T(8,128)(2,1)} fusion(bf16[2,8,16,128,128]{4,3,2,1,0:T(8,128)(2,1)} %pad_maximum_fusion, pred[]{:T(512)S(6)} %eq.81), kind=kLoop, calls=%fused_computation.16 | loop fusion | flops 4194304 | bytes 16777216 | tf_op jit(solution)/shard_map/jit(_where)/select_n | solution.py:23
  598.2 28.2 %subtract_select_fusion = f32[2,128,256,128]{1,3,2,0:T(8,128)} fusion(f32[2,128,256,128]{1,3,2,0:T(8,128)} %copy-done.3, bf16[256,128,128,1]{2,1,0,3:T(8,128)(2,1)} %bitcast.63, f32[2,128,128]{1,2,0:T(8,128)S(1)} %copy.44, pred[256]{0:T(512)(128)(4,1)S(1)} %broadcast_compare_fusion.1, bf16[2,128,128]{2,1,0:T(8,128)(2,1)S(1)} %copy-done.6), kind=kOutput, calls=%fused_computation.6 | convolution fusion | flops 2164260864 | bytes 75694336 | tf_op jit(solution)/shard_map/iac,jcb->iajb/dot_general | solution.py:96
  626.3 31.2 %copy.47 = f32[2,128,256,128]{3,2,1,0:T(8,128)} copy(f32[2,128,256,128]{1,3,2,0:T(8,128)} %subtract_select_fusion) | data formatting | bytes 67108864 | tf_op jit(solution)/shard_map/jit(_where)/select_n | solution.py:104
  657.5 31.8 %copy.58 = f32[32,8,256,128]{3,1,2,0:T(8,128)} copy(f32[32,8,256,128]{3,2,1,0:T(8,128)} %bitcast.62) | data formatting | bytes 67108864
  (26 shorter events, 0.1 us)
Async XLA Ops:
  6.5 281.5 %copy-start = (f32[128,128]{1,0:T(8,128)S(1)}, f32[128,128]{1,0:T(8,128)}, u32[]{:S(2)}) copy-start(f32[128,128]{1,0:T(8,128)} %param.9) | copy-start | bytes 196612
  6.5 132.6 %all-gather.2.cloned.1.call-start = ((), (), s32[]{:S(2)}) async-start(), calls=%async_computation | async-start | bytes 17825792 | tf_op jit(solution)/shard_map/all_gather | solution.py:48
  7.3 221.7 %all-reduce.5.cloned.1.call-start = ((), (), s32[]{:S(2)}) async-start(), calls=%async_computation.1 | async-start | bytes 262144 | tf_op jit(solution)/shard_map/psum | solution.py:67
  149.6 11.7 %copy-start.2 = (f32[256,256,128]{2,1,0:T(8,128)}, f32[256,256,128]{2,1,0:T(8,128)S(1)}, u32[]{:S(2)}) copy-start(f32[256,256,128]{2,1,0:T(8,128)S(1)} %convert_element_type.36) | copy-start | bytes 100663296
  209.1 27.2 %copy-start.8 = (f32[2,128]{1,0:T(2,128)S(1)}, f32[2,128]{1,0:T(2,128)}, u32[]{:S(2)}) copy-start(f32[2,128]{1,0:T(2,128)} %param.8) | copy-start | bytes 3076
  209.2 43.5 %all-reduce.7.cloned.1.call-start = ((), (), s32[]{:S(2)}) async-start(), calls=%async_computation.2 | async-start | bytes 262144 | tf_op jit(solution)/shard_map/psum | solution.py:33
  209.9 100.8 %all-reduce.9.cloned.1.call-start = ((), (), s32[]{:S(2)}) async-start(), calls=%async_computation.3 | async-start | bytes 262144 | tf_op jit(solution)/shard_map/psum | solution.py:33
  228.9 7.5 %copy-start.5 = (f32[2,128,128]{2,1,0:T(8,128)S(1)}, f32[2,128,128]{2,1,0:T(8,128)}, u32[]{:S(2)}) copy-start(f32[2,128,128]{2,1,0:T(8,128)} %all-reduce.5.cloned.1.call-done) | copy-start | bytes 393220
  236.5 52.5 %copy-start.7 = (bf16[16,256]{1,0:T(8,128)(2,1)S(1)}, bf16[16,256]{1,0:T(8,128)(2,1)}, u32[]{:S(2)}) copy-start(bf16[16,256]{1,0:T(8,128)(2,1)} %param.7) | copy-start | bytes 24580
  236.5 74.2 %copy-start.4 = (bf16[16,256,128]{2,1,0:T(8,128)(2,1)S(1)}, bf16[16,256,128]{2,1,0:T(8,128)(2,1)}, u32[]{:S(2)}) copy-start(bf16[16,256,128]{2,1,0:T(8,128)(2,1)} %param.5) | copy-start | bytes 3145732
  276.3 11.7 %copy-start.3 = (f32[2,128,256,128]{1,3,2,0:T(8,128)}, f32[2,128,256,128]{1,3,2,0:T(8,128)S(1)}, u32[]{:S(2)}) copy-start(f32[2,128,256,128]{1,3,2,0:T(8,128)S(1)} %bitcast_select_fusion) | copy-start | bytes 100663296
  312.9 2.0 collective-permute-start
  315.6 25.3 %collective-permute-start.1 = (bf16[2,16,128,128]{3,2,1,0:T(8,128)(2,1)S(1)}, bf16[2,16,128,128]{3,2,1,0:T(8,128)(2,1)S(1)}, u32[]{:S(2)}, u32[]{:S(2)}) collective-permute-start(bf16[2,16,128,128]{3,2,1,0:T(8,128)(2,1)S(1)} %get-tuple-element.8), channel_id=1, source_target_pairs={{0,4},{2,6},{4,0},{6,2},{8,12},{10,14},{12,8},{14,10},{16,20},{18,... | collective-permute-start | bytes 3145736 | tf_op jit(solution)/shard_map/ppermute | solution.py:20
  341.7 47.0 %collective-permute-start.2 = (bf16[4,16,128,128]{3,2,1,0:T(8,128)(2,1)S(1)}, bf16[4,16,128,128]{3,2,1,0:T(8,128)(2,1)}, u32[]{:S(2)}, u32[]{:S(2)}) collective-permute-start(bf16[4,16,128,128]{3,2,1,0:T(8,128)(2,1)S(1)} %bitcast.64), channel_id=1, source_target_pairs={{0,8},{2,10},{4,12},{6,14},{8,0},{10,2},{12,4},{14,6},{16,24},{18,... | collective-permute-start | bytes 6291464 | tf_op jit(solution)/shard_map/ppermute | solution.py:20
  388.7 7.5 %copy-start.6 = (bf16[2,128,128]{2,1,0:T(8,128)(2,1)S(1)}, bf16[2,128,128]{2,1,0:T(8,128)(2,1)}, u32[]{:S(2)}) copy-start(bf16[2,128,128]{2,1,0:T(8,128)(2,1)} %get-tuple-element.5) | copy-start | bytes 196612
  393.8 182.0 %collective-permute-start.3 = (bf16[8,16,128,128]{3,2,1,0:T(8,128)(2,1)}, bf16[8,16,128,128]{3,2,1,0:T(8,128)(2,1)}, u32[]{:S(2)}, u32[]{:S(2)}) collective-permute-start(bf16[8,16,128,128]{3,2,1,0:T(8,128)(2,1)} %bitcast.24), channel_id=1, source_target_pairs={{0,16},{2,18},{4,20},{6,22},{8,24},{10,26},{12,28},{14,30},{16,0},... | collective-permute-start | bytes 12582920 | tf_op jit(solution)/shard_map/ppermute | solution.py:20
  657.5 31.8 %copy-start.1 = (f32[128,128]{1,0:T(8,128)S(1)}, f32[128,128]{1,0:T(8,128)}, u32[]{:S(2)}) copy-start(f32[128,128]{1,0:T(8,128)} %param.9) | copy-start | bytes 196612
Sparse Core Ops, SparseCore 0:
  9.5 129.5 all-gather.1
  209.3 19.5 all-reduce.4
  231.2 21.4 all-reduce.6
  289.1 21.5 all-reduce.8
